TPU v7x, 256 devices: a whole 4x4x8 slice. The times are simulated.
256 devices in a mesh: dp: 32 (over y, z_hi, core), centre: 8 (over x, z_lo).
Axes of the slice: x: 4, y: 4, z: 8 (z_hi: 4, z_lo: 2; z = z_hi * 2 + z_lo), core: 2. Of those that a mesh axis runs over, the one named last changes fastest.
Arguments:
- samples: float32 [16384, 512], P('dp'), may hold values from -4 to 4
- targets: float32 [16384, 64], P('dp'), may hold values from -6 to 6
- centres: float32 [32768, 512], P('centre'), may hold values from -4 to 4
- coefficients: float32 [32768, 64], P('centre'), may hold values from -0.9 to 0.9
Outputs:
- residual: float32 [16384, 64], P('dp')
- new_coefficients: float32 [32768, 64], P(('centre', 'dp'))
All inputs are finite; a program needn't handle non-finite values.
Results may differ from a plain program's by a relative error of at most 0.0001.
Values sent between devices are 32-bit elements; how exact they have to be, the bound alone decides.
A program may use at most 128 MiB of HBM per device.

v0:
```python
import functools
import math

import jax
import jax.numpy as jnp
from jax import lax
from jax.experimental import pallas as pl
from jax.experimental.pallas import tpu as pltpu
from jax.sharding import PartitionSpec as P

MESH = pl.DeviceIdType.MESH
f32, bf16 = jnp.float32, jnp.bfloat16
NT = (((1,), (1,)), ((), ()))

SOFTENING = 0.01
KERNEL_SCALE = 0.2
LEARNING_RATE = 4.0
SCALE_SQ = (math.log2(math.e) / KERNEL_SCALE) ** 2
EPS = SOFTENING * SCALE_SQ

PAIRS = ((0, 0), (1, 0), (3, 0), (2, 0), (0, 1), (1, 1), (3, 1), (2, 1))
PLACE = {pair: at for at, pair in enumerate(PAIRS)}
FIRST_ROWS = ((1, 0), (3, 0), (0, 1))
LATER_ROWS = ((1, 1), (3, 1))
SUM_TOP = 40
TOP = 48


def halves(x):
    hi = x.astype(bf16)
    lo = (x - hi.astype(f32)).astype(bf16)
    return hi, lo


def kernel_of(z):
    z = jnp.maximum(z, EPS)
    return jnp.exp2(-(z * lax.rsqrt(z)))


def lanes(x, times):
    return jnp.concatenate([x] * times, axis=1)


def near_first(t):
    return t + t // 2 - 2 * (t // 3)


def loop(start, stop, f):
    def step(i, _):
        f(i)
        return 0

    lax.fori_loop(start, stop, step, 0)


def step_kernel(
    samples, targets, centres, coefs, res_out, new_out,
    cen, cof, smp, tgt, rows,
    c3, ccol, crow, s3, scol, r3, rrow, cof2,
    kh, kl, th, tl,
    pacc, pred, pred_in, res,
    gpart, g_y, gsum, g_z, h_z, hsum, h_y,
    whole, part, other, summed, arrived, lhs_r, lhs_u,
    loc_sem, smp_send, smp_recv, row_send, row_recv, fwd_send, fwd_recv, rel_send, rel_recv,
    p_send, p_recv, q_send, q_recv,
    gy_send, gy_recv, gz_send, gz_recv, hz_send, hz_recv, hy_send, hy_recv,
    a_send, a_recv, b_send, b_recv, c_send, c_recv, o_send, o_recv,
):
    n = 128
    d, c = lax.axis_index("dp"), lax.axis_index("centre")
    core, zh, y = d % 2, (d // 2) % 4, d // 8
    x, zl = c // 2, c % 2
    sib = d + 1 - 2 * core
    mine = pl.ds(pl.multiple_of(c * 8, 8), 8)
    own_rows = pl.ds(pl.multiple_of(d * n, n), n)
    sib_rows = pl.ds(pl.multiple_of(sib * n, n), n)

    def at_y(j):
        return (((y + j) % 4 * 4 + zh) * 2 + core, c)

    def at_z(j):
        return ((y * 4 + (zh + j) % 4) * 2 + core, c)

    def centre_of(dx, dz):
        return (x + dx) % 4 * 2 + (zl + dz) % 2

    def remote(src, dst, send, recv, to):
        return pltpu.make_async_remote_copy(
            src_ref=src, dst_ref=dst, send_sem=send, recv_sem=recv, device_id=to, device_id_type=MESH
        )

    def got(like, sem):
        remote(like, like, sem, sem, (sib, c)).wait_recv()

    def sent(like, sem):
        remote(like, like, sem, sem, (sib, c)).wait_send()

    def block_loads(b):
        owner = ((y + b // 4) % 4 * 4 + (zh + b % 4) % 4) * 2 + core
        at = pl.ds(pl.multiple_of(owner * n, n), n)
        to = pl.ds(pl.multiple_of(b * n, n), n)
        return (
            pltpu.make_async_copy(centres.at[at], cen.at[to], loc_sem.at[4 + b]),
            pltpu.make_async_copy(coefs.at[:, at], cof.at[:, to], loc_sem.at[20 + b]),
        )

    smp_load = pltpu.make_async_copy(samples, smp.at[0], loc_sem.at[0])
    late_loads = (
        pltpu.make_async_copy(targets, tgt, loc_sem.at[1]),
        pltpu.make_async_copy(centres.at[own_rows], rows.at[0, 0], loc_sem.at[2]),
        pltpu.make_async_copy(centres.at[sib_rows], rows.at[0, 1], loc_sem.at[3]),
    )
    smp_load.start()

    @functools.partial(loop, 0, 16)
    def _(b):
        for copy in block_loads(b):
            copy.start()

    for copy in late_loads:
        copy.start()

    barrier = pltpu.get_barrier_semaphore()
    partners = [(sib, c)] + [at_y(j) for j in (1, 2, 3)] + [at_z(j) for j in (1, 2, 3)]
    for dx, dz in PAIRS[1:]:
        partners += [(d, centre_of(dx, dz)), (sib, centre_of(dx, dz))]
    for to in partners:
        pl.semaphore_signal(barrier, inc=1, device_id=to, device_id_type=MESH)

    def send_rows(pairs):
        for dx, dz in pairs:
            j = PLACE[((4 - dx) % 4, dz)]
            remote(
                cen.at[pl.ds(0, n)], rows.at[j, 0], row_send.at[PLACE[(dx, dz)]], row_recv.at[j], (d, centre_of(dx, dz))
            ).start()

    def relay_rows(dz):
        far = PLACE[(2, dz)]
        for i, (back, on) in enumerate(((1, 3), (3, 1))):
            half = pl.ds(i * 64, 64)
            remote(
                rows.at[PLACE[(back, dz)], 0, half], rows.at[far, 0, half],
                rel_send.at[dz * 2 + i], rel_recv.at[dz * 2 + i], (d, centre_of(on, 0)),
            ).start()

    def await_relayed(dz):
        for i in (0, 1):
            got(rows.at[PLACE[(2, dz)], 0, pl.ds(i * 64, 64)], rel_recv.at[dz * 2 + i])

    def forward_rows(j):
        remote(rows.at[j, 0], rows.at[j, 1], fwd_send.at[j], fwd_recv.at[j], (sib, c)).start()

    def pass_on(pairs, dz):
        for pair in pairs:
            got(rows.at[PLACE[pair], 0], row_recv.at[PLACE[pair]])
        relay_rows(dz)
        for pair in pairs:
            forward_rows(PLACE[pair])

    def norm_of(v):
        total = jnp.sum(v * v, axis=1, keepdims=True) * SCALE_SQ
        return jnp.broadcast_to(total, (n, n))

    def prepare_samples(half):
        @functools.partial(loop, 0, 4)
        def _(i):
            at = pl.ds(pl.multiple_of(i * n, n), n)
            to = pl.ds(pl.multiple_of(half * 512 + i * n, n), n)
            v = smp[half, at, :]
            hi, lo = halves(v * (-2.0 * SCALE_SQ))
            s3[to, 0:512] = hi
            s3[to, 512:1024] = hi
            s3[to, 1024:1536] = lo
            scol[to, :] = norm_of(v) + EPS

    smp_load.wait()
    prepare_samples(0)

    @functools.partial(loop, 0, 16)
    def _(b):
        for copy in block_loads(b):
            copy.wait()
        at = pl.ds(pl.multiple_of(b * n, n), n)
        v = cen[at, :]
        hi, lo = halves(v)
        c3[at, 0:512] = hi
        c3[at, 512:1024] = lo
        c3[at, 1024:1536] = hi
        norms = norm_of(v)
        ccol[at, :] = norms + EPS
        crow[:, at] = norms.T[0:8, :]
        w = cof[:, at]
        whi = w.astype(bf16).astype(f32)
        cof2[at, :] = jnp.concatenate([whi, w - whi], axis=0).T.astype(bf16)

        @pl.when(b == 5)
        def _():
            pl.semaphore_wait(barrier, len(partners))
            for i in range(4):
                at = pl.ds(i * n, n)
                remote(smp.at[0, at], smp.at[1, at], smp_send.at[i], smp_recv.at[i], (sib, c)).start()
            send_rows(FIRST_ROWS)

    tn = 512
    pacc[...] = jnp.zeros_like(pacc)

    @functools.partial(loop, 0, 8)
    def _(i):
        @pl.when(i == 4)
        def _():
            for k in range(4):
                got(smp.at[1, pl.ds(k * n, n)], smp_recv.at[k])
            prepare_samples(1)

        @pl.when(i == 6)
        def _():
            pass_on(FIRST_ROWS, 0)

        these = pl.ds(pl.multiple_of(i // 4 * 512, 512), 512)
        at = pl.ds(pl.multiple_of(i % 4 * tn, tn), tn)
        cross = lax.dot_general(s3[these, :], c3[at, :], NT, preferred_element_type=f32)
        value = kernel_of(cross + lanes(scol[these, :], tn // n) + crow[0:1, at])
        hi, lo = halves(value)
        kh[these, at] = hi
        kl[these, at] = lo
        w = cof2[at, :]
        pacc[these, :] += jnp.dot(hi, w, preferred_element_type=f32) + jnp.dot(lo, w, preferred_element_type=f32)

    both = pacc[...].T
    pred[...] = both[0:64] + both[64:128]

    def member(s):
        dx, dz, kk = s // 4, s // 2 % 2, s % 2
        return centre_of(dx, dz), d + kk * (sib - d), kk

    @functools.partial(loop, 1, 16)
    def _(s):
        to, at_d, kk = member(s)
        remote(
            pred.at[pl.ds(pl.multiple_of(to * 8, 8), 8), pl.ds(pl.multiple_of(kk * 512, 512), 512)],
            pred_in.at[s - 1], p_send.at[s - 1], p_recv.at[s - 1], (at_d, to),
        ).start()

    for copy in late_loads:
        copy.wait()

    def residuals():
        loop(0, 15, lambda s: got(pred_in.at[s], p_recv.at[s]))
        total = pred[mine, 0:512] - tgt[mine, :]
        for s in range(15):
            total += pred_in[s]
        res[0, mine, :] = total

        @functools.partial(loop, 1, 16)
        def _(s):
            to, at_d, kk = member(s)
            remote(res.at[0, mine], res.at[kk, mine], q_send.at[s - 1], q_recv.at[s - 1], (at_d, to)).start()

        await_relayed(0)
        forward_rows(PLACE[(2, 0)])
        got(rows.at[1, 0], fwd_recv.at[1])
        got(rows.at[2, 0], fwd_recv.at[2])

    top, low = pl.ds(0, SUM_TOP), pl.ds(SUM_TOP, 64 - SUM_TOP)

    def gradients():
        loop(0, 15, lambda s: got(res.at[0, pl.ds(0, 8)], q_recv.at[s]))
        send_rows(LATER_ROWS)
        for kk in (0, 1):
            hi, lo = halves(res[kk])
            lhs_r[0:64, kk * 512 : kk * 512 + 512] = lo
            lhs_r[64:128, kk * 512 : kk * 512 + 512] = hi

        @functools.partial(loop, 0, 4)
        def _(t):
            dy = (t + 1) % 4
            at = pl.ds(pl.multiple_of(dy * 512, 512), 512)
            a = jnp.dot(lhs_r[...], kh[:, at], preferred_element_type=f32)
            b = jnp.dot(lhs_r[64:128, :], kl[:, at], preferred_element_type=f32)
            gpart[dy] = a[0:64] + a[64:128] + b

            @pl.when(t < 3)
            def _():
                remote(gpart.at[dy, top], g_y.at[t], gy_send.at[t], gy_recv.at[t], at_y(t + 1)).start()

        for j in (1, 2, 3):
            remote(
                gpart.at[:, low, pl.ds(j * n, n)], h_z.at[j - 1], hz_send.at[j - 1], hz_recv.at[j - 1], at_z(j)
            ).start()
        res_out[...] = res[0]
        got(rows.at[3, 0], fwd_recv.at[3])
        got(rows.at[4, 0], fwd_recv.at[4])

    first, rest = pl.ds(0, TOP), pl.ds(TOP, 72 - TOP)
    start = pl.ds(0, n)

    def spread_first(it):
        for j in (1, 2, 3):
            to = 4 - j
            remote(
                whole.at[it, 0, first, start], whole.at[it, 0, first, pl.ds(to * n, n)],
                a_send.at[it, j - 1], a_recv.at[it, j - 1], at_z(j),
            ).start()
            remote(
                whole.at[it, 0, rest, start], whole.at[it, to, rest, start],
                a_send.at[it, j + 2], a_recv.at[it, j + 2], at_y(j),
            ).start()

    def spread_more(it):
        for j in (1, 2, 3):
            got(whole.at[it, 0, rest, start], a_recv.at[it, j + 2])
        for j in (1, 2, 3):
            to = 4 - j
            remote(
                whole.at[it, :, rest, start], whole.at[it, :, rest, pl.ds(to * n, n)],
                b_send.at[it, j - 1], b_recv.at[it, j - 1], at_z(j),
            ).start()
        for j in (1, 2, 3):
            got(whole.at[it, 0, first, start], a_recv.at[it, j - 1])
        for j in (1, 2, 3):
            remote(
                whole.at[it, 0, first], whole.at[it, 4 - j, first],
                b_send.at[it, j + 2], b_recv.at[it, j + 2], at_y(j),
            ).start()

    def sum_gradients():
        for j in range(3):
            got(g_y.at[j], gy_recv.at[j])
        gsum[...] = gpart[0, 0:SUM_TOP] + g_y[0] + g_y[1] + g_y[2]
        for j in (1, 2, 3):
            remote(
                gsum.at[:, pl.ds(j * n, n)], g_z.at[j - 1], gz_send.at[j - 1], gz_recv.at[j - 1], at_z(j)
            ).start()
        for j in range(3):
            got(h_z.at[j], hz_recv.at[j])
        hsum[...] = gpart[:, SUM_TOP:64, 0:n] + h_z[0] + h_z[1] + h_z[2]
        for j in (1, 2, 3):
            remote(hsum.at[j], h_y.at[j - 1], hy_send.at[j - 1], hy_recv.at[j - 1], at_y(j)).start()
        pass_on(LATER_ROWS, 1)
        for j in range(3):
            got(g_z.at[j], gz_recv.at[j])
            got(h_y.at[j], hy_recv.at[j])
        whole[0, 0, 0:SUM_TOP, 0:n] = gsum[:, 0:n] + g_z[0] + g_z[1] + g_z[2]
        whole[0, 0, SUM_TOP:64, 0:n] = hsum[0] + h_y[0] + h_y[1] + h_y[2]
        whole[0, 0, 64:72, 0:n] = jnp.zeros((8, n), f32)
        spread_first(0)
        got(rows.at[5, 0], fwd_recv.at[5])

    def spread_gradients():
        spread_more(0)
        await_relayed(1)
        forward_rows(7)
        got(rows.at[6, 0], fwd_recv.at[6])

    tm = 1024

    @functools.partial(loop, 0, 8)
    def _(j):
        for kk in (0, 1):
            v = rows[j, kk]
            hi, lo = halves(v * (-2.0 * SCALE_SQ))
            to = slice(kk * n, kk * n + n)
            r3[to, 0:512] = hi
            r3[to, 512:1024] = hi
            r3[to, 1024:1536] = lo
            rrow[:, to] = norm_of(v).T[0:8, :]
        cols = pl.ds(pl.multiple_of(j * 256, 256), 256)

        @functools.partial(loop, 0, 2048 // tm)
        def _(i):
            at = pl.ds(pl.multiple_of(i * tm, tm), tm)
            cross = lax.dot_general(c3[at, :], r3[...], NT, preferred_element_type=f32)
            hi, lo = halves(kernel_of(cross + lanes(ccol[at, :], 2) + rrow[0:1, :]))
            th[at, cols] = hi
            tl[at, cols] = lo

        pl.when(j == 0)(residuals)
        pl.when(j == 2)(gradients)
        pl.when(j == 4)(sum_gradients)
        pl.when(j == 5)(spread_gradients)

        @pl.when(j == 6)
        def _():
            got(rows.at[7, 0], fwd_recv.at[7])

    lhs_u[128:144, :] = jnp.ones((16, 512), bf16)
    part[...] = jnp.zeros_like(part)

    @functools.partial(loop, 0, 2)
    def _(it):
        @functools.partial(loop, 0, 4)
        def _(t):
            dy = near_first(t)

            @pl.when(t == 0)
            def _():
                for j in range(3):
                    got(whole.at[0, :, rest, start], b_recv.at[it, j])

            @pl.when(t > 0)
            def _():
                got(whole.at[0, 0, first], b_recv.at[it, 6 - dy])

            hi, lo = halves(whole[it, dy, 0:64, :])
            lhs_u[0:64, :] = lo
            lhs_u[64:128, :] = hi
            k = pl.ds(pl.multiple_of(dy * 512, 512), 512)

            @functools.partial(loop, 0, 4)
            def _(back):
                i = 3 - back
                at = pl.ds(pl.multiple_of(i * 512, 512), 512)
                a = jnp.dot(lhs_u[...], th[k, at], preferred_element_type=f32)
                b = jnp.dot(lhs_u[64:144, :], tl[k, at], preferred_element_type=f32)
                part[it, 0:64, at] += a[0:64] + a[64:128] + b[0:64]
                part[it, 64:72, at] += a[128:136] + b[64:72]

                @pl.when(t == 3)
                def _():
                    @pl.when(it == 1)
                    def _():
                        largest = whole[1, 0, 64:72, 0:n]
                        for e in range(1, 16):
                            largest = jnp.maximum(largest, whole[1, e // 4, 64:72, e % 4 * n : e % 4 * n + n])
                        largest = lanes(largest, 4)
                        part[1, 64:72, at] = largest

                    for j in (2 * i + 1, 2 * i):
                        theirs = pl.ds(pl.multiple_of((2 * j + 1) * n, n), n)
                        remote(
                            part.at[it, :, theirs], other.at[it, j], c_send.at[it, j], c_recv.at[it, j], (sib, c)
                        ).start()

        def added(a, b):
            return jnp.concatenate([a[0:64] + b[0:64], jnp.where(it == 1, jnp.maximum(a[64:72], b[64:72]), a[64:72] + b[64:72])])

        @functools.partial(loop, 0, 8)
        def _(back):
            j = 7 - back
            got(other.at[0, 0], c_recv.at[it, j])
            ours = pl.ds(pl.multiple_of(2 * j * n, n), n)
            summed[it, j] = added(part[it, :, ours], other[it, j])

            @pl.when(j > 0)
            def _():
                to = centre_of(near_first(j % 4), j // 4)
                remote(
                    summed.at[it, j], arrived.at[it, j - 1], o_send.at[it, j - 1], o_recv.at[it, j - 1], (d, to)
                ).start()

        loop(0, 7, lambda s: got(arrived.at[0, 0], o_recv.at[it, s]))
        total = summed[it, 0]
        for s in range(7):
            total = added(total, arrived[it, s])

        @pl.when(it == 0)
        def _():
            whole[1, 0, 0:64, 0:n] = total[0:64]
            whole[1, 0, 64:72, 0:n] = jnp.broadcast_to(jnp.max(total[64:72], axis=1, keepdims=True), (8, n))
            spread_first(1)
            spread_more(1)

        @pl.when(it == 1)
        def _():
            size = jnp.concatenate([1.0 / total[64:72]] * 8, axis=0)
            once, grad = whole[1, 0, 0:64, 0:n], whole[0, 0, 0:64, 0:n]
            theta = size * (3.0 * grad - size * (3.0 * once - size * total[0:64]))
            new_out[...] = cof[:, 0:n] - LEARNING_RATE * theta

    for i in range(4):
        sent(smp.at[0, pl.ds(0, n)], smp_send.at[i])
        sent(rows.at[0, 0, pl.ds(0, 64)], rel_send.at[i])
    for pair in FIRST_ROWS + LATER_ROWS:
        sent(rows.at[0, 0], row_send.at[PLACE[pair]])
    loop(1, 8, lambda j: sent(rows.at[0, 0], fwd_send.at[j]))

    @functools.partial(loop, 0, 15)
    def _(s):
        sent(pred_in.at[0], p_send.at[s])
        sent(pred_in.at[0], q_send.at[s])

    @functools.partial(loop, 0, 3)
    def _(j):
        sent(g_y.at[0], gy_send.at[j])
        sent(g_z.at[0], gz_send.at[j])
        sent(h_z.at[0], hz_send.at[j])
        sent(h_y.at[0], hy_send.at[j])
        for it in (0, 1):
            sent(whole.at[0, 0, first, start], a_send.at[it, j])
            sent(whole.at[0, 0, rest, start], a_send.at[it, j + 3])
            sent(whole.at[0, :, rest, start], b_send.at[it, j])
            sent(whole.at[0, 0, first], b_send.at[it, j + 3])

    @functools.partial(loop, 0, 8)
    def _(j):
        for it in (0, 1):
            sent(other.at[0, 0], c_send.at[it, j])

            @pl.when(j > 0)
            def _():
                sent(other.at[0, 0], o_send.at[it, j - 1])


def hand_over(res_in, new_in, res_out, new_out):
    res_out[...] = res_in[...]
    new_out[...] = new_in[...]


def body(samples, targets, centres, coefficients):
    dma = pltpu.SemaphoreType.DMA
    vmem = pltpu.VMEM
    res_t, new_t = pl.pallas_call(
        step_kernel,
        out_shape=(jax.ShapeDtypeStruct((64, 512), f32), jax.ShapeDtypeStruct((64, 128), f32)),
        in_specs=[pl.BlockSpec(memory_space=pl.ANY)] * 4,
        out_specs=[pl.BlockSpec(memory_space=vmem)] * 2,
        scratch_shapes=[
            vmem((2048, 512), f32), vmem((64, 2048), f32), vmem((2, 512, 512), f32), vmem((64, 512), f32),
            vmem((8, 2, 128, 512), f32),
            vmem((2048, 1536), bf16), vmem((2048, 128), f32), vmem((8, 2048), f32),
            vmem((1024, 1536), bf16), vmem((1024, 128), f32), vmem((256, 1536), bf16), vmem((8, 256), f32),
            vmem((2048, 128), bf16),
            vmem((1024, 2048), bf16), vmem((1024, 2048), bf16), vmem((2048, 2048), bf16), vmem((2048, 2048), bf16),
            vmem((1024, 128), f32), vmem((64, 1024), f32), vmem((15, 8, 512), f32), vmem((2, 64, 512), f32),
            vmem((4, 64, 512), f32), vmem((3, SUM_TOP, 512), f32), vmem((SUM_TOP, 512), f32), vmem((3, SUM_TOP, 128), f32),
            vmem((3, 4, 64 - SUM_TOP, 128), f32), vmem((4, 64 - SUM_TOP, 128), f32), vmem((3, 64 - SUM_TOP, 128), f32),
            vmem((2, 4, 72, 512), f32), vmem((2, 72, 2048), f32), vmem((2, 8, 72, 128), f32), vmem((2, 8, 72, 128), f32),
            vmem((2, 7, 72, 128), f32), vmem((128, 1024), bf16), vmem((144, 512), bf16),
            dma((36,)), dma((4,)), dma((4,)), dma((8,)), dma((8,)), dma((8,)), dma((8,)), dma((4,)), dma((4,)),
            dma((15,)), dma((15,)), dma((15,)), dma((15,)),
            dma((3,)), dma((3,)), dma((3,)), dma((3,)), dma((3,)), dma((3,)), dma((3,)), dma((3,)),
            dma((2, 6)), dma((2, 6)), dma((2, 6)), dma((2, 6)),
            dma((2, 8)), dma((2, 8)), dma((2, 7)), dma((2, 7)),
        ],
        compiler_params=pltpu.CompilerParams(
            collective_id=0, has_side_effects=True, vmem_limit_bytes=63 * 2**20
        ),
    )(samples, targets.T, centres, coefficients.T)
    res_t, new_t = pl.pallas_call(
        hand_over,
        out_shape=(jax.ShapeDtypeStruct((64, 512), f32), jax.ShapeDtypeStruct((64, 128), f32)),
        in_specs=[pl.BlockSpec(memory_space=vmem)] * 2,
        out_specs=[pl.BlockSpec(memory_space=vmem)] * 2,
    )(res_t, new_t)
    return res_t.T, new_t.T


def solution(mesh):
    return jax.shard_map(
        body,
        mesh=mesh,
        in_specs=(P("dp", None), P("dp", None), P("centre", None), P("centre", None)),
        out_specs=(P("dp", None), P(("centre", "dp"), None)),
        check_vma=False,
    )
```

profile of v0, /device:TPU:1, one launch (start us, length us, event | category | flops | bytes accessed | tf_op | source)
XLA Modules:
  0.0 110.1 jit_solution(10756830460185880155)
XLA Ops:
  0.6 107.9 %shard_map.59 = (f32[64,512]{1,0:T(8,128)}, f32[64,128]{1,0:T(8,128)}) custom-call(f32[512,512]{1,0:T(8,128)} %samples.1, f32[64,512]{1,0:T(8,128)} %bitcast.5, f32[4096,512]{1,0:T(8,128)} %centres.1, f32[64,4096]{1,0:T(8,128)} %bitcast.4), custom_call_target="tpu_custom_call" | custom-call | tf_op jit(solution)/shard_map/pallas_call | solution.py:512
  108.5 1.6 %shard_map.60 = (f32[64,512]{1,0:T(8,128)}, f32[64,128]{1,0:T(8,128)}) custom-call(f32[64,512]{1,0:T(8,128)} %get-tuple-element.6.res_in, f32[64,128]{1,0:T(8,128)} %get-tuple-element.7.new_in), custom_call_target="tpu_custom_call" | custom-call | tf_op jit(solution)/shard_map/pallas_call | solution.py:539
where the time goes:
time: 110 us
  Pallas kernels  109 us (99%)
    pallas_call x1, Pallas kernels, body(): pl.pallas_call(step_kernel, out_shape=(jax.ShapeDtypeStruct((64, 512), f3...  108 us

commit v1 on v0

--- a/solution.py
+++ b/solution.py
@@ -193,31 +193,27 @@
         whi = w.astype(bf16).astype(f32)
         cof2[at, :] = jnp.concatenate([whi, w - whi], axis=0).T.astype(bf16)
 
-        @pl.when(b == 5)
+    tn = 1024
+    pacc[...] = jnp.zeros_like(pacc)
+
+    @functools.partial(loop, 0, 4)
+    def _(i):
+        @pl.when(i == 1)
         def _():
             pl.semaphore_wait(barrier, len(partners))
-            for i in range(4):
-                at = pl.ds(i * n, n)
-                remote(smp.at[0, at], smp.at[1, at], smp_send.at[i], smp_recv.at[i], (sib, c)).start()
+            for k in range(4):
+                at = pl.ds(k * n, n)
+                remote(smp.at[0, at], smp.at[1, at], smp_send.at[k], smp_recv.at[k], (sib, c)).start()
             send_rows(FIRST_ROWS)
 
-    tn = 512
-    pacc[...] = jnp.zeros_like(pacc)
-
-    @functools.partial(loop, 0, 8)
-    def _(i):
-        @pl.when(i == 4)
+        @pl.when(i == 2)
         def _():
             for k in range(4):
                 got(smp.at[1, pl.ds(k * n, n)], smp_recv.at[k])
             prepare_samples(1)
 
-        @pl.when(i == 6)
-        def _():
-            pass_on(FIRST_ROWS, 0)
-
-        these = pl.ds(pl.multiple_of(i // 4 * 512, 512), 512)
-        at = pl.ds(pl.multiple_of(i % 4 * tn, tn), tn)
+        these = pl.ds(pl.multiple_of(i // 2 * 512, 512), 512)
+        at = pl.ds(pl.multiple_of(i % 2 * tn, tn), tn)
         cross = lax.dot_general(s3[these, :], c3[at, :], NT, preferred_element_type=f32)
         value = kernel_of(cross + lanes(scol[these, :], tn // n) + crow[0:1, at])
         hi, lo = halves(value)
@@ -243,6 +239,7 @@
 
     for copy in late_loads:
         copy.wait()
+    pass_on(FIRST_ROWS, 0)
 
     def residuals():
         loop(0, 15, lambda s: got(pred_in.at[s], p_recv.at[s]))
@@ -265,7 +262,12 @@
 
     def gradients():
         loop(0, 15, lambda s: got(res.at[0, pl.ds(0, 8)], q_recv.at[s]))
-        send_rows(LATER_ROWS)
+        for dx in (1, 3):
+            j = PLACE[(4 - dx, 1)]
+            remote(
+                rows.at[PLACE[(0, 1)], 0], rows.at[j, 0], row_send.at[PLACE[(dx, 1)]], row_recv.at[j],
+                (d, centre_of(dx, 0)),
+            ).start()
         for kk in (0, 1):
             hi, lo = halves(res[kk])
             lhs_r[0:64, kk * 512 : kk * 512 + 512] = lo
@@ -352,7 +354,6 @@
         forward_rows(7)
         got(rows.at[6, 0], fwd_recv.at[6])
 
-    tm = 1024
 
     @functools.partial(loop, 0, 8)
     def _(j):
@@ -366,13 +367,10 @@
             rrow[:, to] = norm_of(v).T[0:8, :]
         cols = pl.ds(pl.multiple_of(j * 256, 256), 256)
 
-        @functools.partial(loop, 0, 2048 // tm)
-        def _(i):
-            at = pl.ds(pl.multiple_of(i * tm, tm), tm)
-            cross = lax.dot_general(c3[at, :], r3[...], NT, preferred_element_type=f32)
-            hi, lo = halves(kernel_of(cross + lanes(ccol[at, :], 2) + rrow[0:1, :]))
-            th[at, cols] = hi
-            tl[at, cols] = lo
+        cross = lax.dot_general(c3[...], r3[...], NT, preferred_element_type=f32)
+        hi, lo = halves(kernel_of(cross + lanes(ccol[...], 2) + rrow[0:1, :]))
+        th[:, cols] = hi
+        tl[:, cols] = lo
 
         pl.when(j == 0)(residuals)
         pl.when(j == 2)(gradients)

time: 110 us -> 98.7 us (0.90)
  Pallas kernels: 109 us -> 98 us
    pallas_call x1, Pallas kernels: 108 us -> 96.4 us  [body(): pl.pallas_call(step_kernel, out_shape=(jax.ShapeDtypeStruct((64, 512), f3...]
where the time goes in v1:
time: 98.7 us; the launch traced here: 98.6 us
  Pallas kernels  98 us (99%)
    pallas_call x1, Pallas kernels, body(): pl.pallas_call(step_kernel, out_shape=(jax.ShapeDtypeStruct((64, 512), f3...  96.4 us

profile of v1, /device:TPU:1, one launch (start us, length us, event | category | flops | bytes accessed | tf_op | source)
XLA Modules:
  0.0 98.6 jit_solution(16973291274108095569)
XLA Ops:
  0.6 96.4 %shard_map.59 = (f32[64,512]{1,0:T(8,128)}, f32[64,128]{1,0:T(8,128)}) custom-call(f32[512,512]{1,0:T(8,128)} %samples.1, f32[64,512]{1,0:T(8,128)} %bitcast.5, f32[4096,512]{1,0:T(8,128)} %centres.1, f32[64,4096]{1,0:T(8,128)} %bitcast.4), custom_call_target="tpu_custom_call" | custom-call | tf_op jit(solution)/shard_map/pallas_call | solution.py:510
  97.1 1.6 %shard_map.60 = (f32[64,512]{1,0:T(8,128)}, f32[64,128]{1,0:T(8,128)}) custom-call(f32[64,512]{1,0:T(8,128)} %get-tuple-element.6.res_in, f32[64,128]{1,0:T(8,128)} %get-tuple-element.7.new_in), custom_call_target="tpu_custom_call" | custom-call | tf_op jit(solution)/shard_map/pallas_call | solution.py:537

commit v2 on v1

--- a/solution.py
+++ b/solution.py
@@ -193,6 +193,23 @@
         whi = w.astype(bf16).astype(f32)
         cof2[at, :] = jnp.concatenate([whi, w - whi], axis=0).T.astype(bf16)
 
+    def member(s):
+        dx, dz, kk = s // 4, s // 2 % 2, s % 2
+        return centre_of(dx, dz), d + kk * (sib - d), kk
+
+    def send_predictions(kk):
+        both = pacc[kk * 512 : kk * 512 + 512, :].T
+        pred[kk] = both[0:64] + both[64:128]
+
+        @functools.partial(loop, 1 - kk, 8)
+        def _(half):
+            s = 2 * half + kk
+            to, at_d, _ = member(s)
+            remote(
+                pred.at[kk, pl.ds(pl.multiple_of(to * 8, 8), 8)],
+                pred_in.at[s - 1], p_send.at[s - 1], p_recv.at[s - 1], (at_d, to),
+            ).start()
+
     tn = 1024
     pacc[...] = jnp.zeros_like(pacc)
 
@@ -211,6 +228,7 @@
             for k in range(4):
                 got(smp.at[1, pl.ds(k * n, n)], smp_recv.at[k])
             prepare_samples(1)
+            send_predictions(0)
 
         these = pl.ds(pl.multiple_of(i // 2 * 512, 512), 512)
         at = pl.ds(pl.multiple_of(i % 2 * tn, tn), tn)
@@ -222,28 +240,14 @@
         w = cof2[at, :]
         pacc[these, :] += jnp.dot(hi, w, preferred_element_type=f32) + jnp.dot(lo, w, preferred_element_type=f32)
 
-    both = pacc[...].T
-    pred[...] = both[0:64] + both[64:128]
-
-    def member(s):
-        dx, dz, kk = s // 4, s // 2 % 2, s % 2
-        return centre_of(dx, dz), d + kk * (sib - d), kk
-
-    @functools.partial(loop, 1, 16)
-    def _(s):
-        to, at_d, kk = member(s)
-        remote(
-            pred.at[pl.ds(pl.multiple_of(to * 8, 8), 8), pl.ds(pl.multiple_of(kk * 512, 512), 512)],
-            pred_in.at[s - 1], p_send.at[s - 1], p_recv.at[s - 1], (at_d, to),
-        ).start()
-
+    send_predictions(1)
     for copy in late_loads:
         copy.wait()
     pass_on(FIRST_ROWS, 0)
 
     def residuals():
         loop(0, 15, lambda s: got(pred_in.at[s], p_recv.at[s]))
-        total = pred[mine, 0:512] - tgt[mine, :]
+        total = pred[0, mine, :] - tgt[mine, :]
         for s in range(15):
             total += pred_in[s]
         res[0, mine, :] = total
@@ -253,6 +257,12 @@
             to, at_d, kk = member(s)
             remote(res.at[0, mine], res.at[kk, mine], q_send.at[s - 1], q_recv.at[s - 1], (at_d, to)).start()
 
+        for dx in (1, 3):
+            j = PLACE[(4 - dx, 1)]
+            remote(
+                rows.at[PLACE[(0, 1)], 0], rows.at[j, 0], row_send.at[PLACE[(dx, 1)]], row_recv.at[j],
+                (d, centre_of(dx, 0)),
+            ).start()
         await_relayed(0)
         forward_rows(PLACE[(2, 0)])
         got(rows.at[1, 0], fwd_recv.at[1])
@@ -262,12 +272,6 @@
 
     def gradients():
         loop(0, 15, lambda s: got(res.at[0, pl.ds(0, 8)], q_recv.at[s]))
-        for dx in (1, 3):
-            j = PLACE[(4 - dx, 1)]
-            remote(
-                rows.at[PLACE[(0, 1)], 0], rows.at[j, 0], row_send.at[PLACE[(dx, 1)]], row_recv.at[j],
-                (d, centre_of(dx, 0)),
-            ).start()
         for kk in (0, 1):
             hi, lo = halves(res[kk])
             lhs_r[0:64, kk * 512 : kk * 512 + 512] = lo
@@ -338,7 +342,6 @@
         hsum[...] = gpart[:, SUM_TOP:64, 0:n] + h_z[0] + h_z[1] + h_z[2]
         for j in (1, 2, 3):
             remote(hsum.at[j], h_y.at[j - 1], hy_send.at[j - 1], hy_recv.at[j - 1], at_y(j)).start()
-        pass_on(LATER_ROWS, 1)
         for j in range(3):
             got(g_z.at[j], gz_recv.at[j])
             got(h_y.at[j], hy_recv.at[j])
@@ -374,6 +377,11 @@
 
         pl.when(j == 0)(residuals)
         pl.when(j == 2)(gradients)
+
+        @pl.when(j == 3)
+        def _():
+            pass_on(LATER_ROWS, 1)
+
         pl.when(j == 4)(sum_gradients)
         pl.when(j == 5)(spread_gradients)
 
@@ -519,7 +527,7 @@
             vmem((1024, 1536), bf16), vmem((1024, 128), f32), vmem((256, 1536), bf16), vmem((8, 256), f32),
             vmem((2048, 128), bf16),
             vmem((1024, 2048), bf16), vmem((1024, 2048), bf16), vmem((2048, 2048), bf16), vmem((2048, 2048), bf16),
-            vmem((1024, 128), f32), vmem((64, 1024), f32), vmem((15, 8, 512), f32), vmem((2, 64, 512), f32),
+            vmem((1024, 128), f32), vmem((2, 64, 512), f32), vmem((15, 8, 512), f32), vmem((2, 64, 512), f32),
             vmem((4, 64, 512), f32), vmem((3, SUM_TOP, 512), f32), vmem((SUM_TOP, 512), f32), vmem((3, SUM_TOP, 128), f32),
             vmem((3, 4, 64 - SUM_TOP, 128), f32), vmem((4, 64 - SUM_TOP, 128), f32), vmem((3, 64 - SUM_TOP, 128), f32),
             vmem((2, 4, 72, 512), f32), vmem((2, 72, 2048), f32), vmem((2, 8, 72, 128), f32), vmem((2, 8, 72, 128), f32),

time: 98.7 us -> 97.3 us (0.986)
  Pallas kernels: 98 us -> 96.6 us
    pallas_call x1, Pallas kernels: 96.4 us -> 95 us  [body(): pl.pallas_call(step_kernel, out_shape=(jax.ShapeDtypeStruct((64, 512), f3...]
where the time goes in v2:
time: 97.3 us; the launch traced here: 97.2 us
  Pallas kernels  96.6 us (99%)
    pallas_call x1, Pallas kernels, body(): pl.pallas_call(step_kernel, out_shape=(jax.ShapeDtypeStruct((64, 512), f3...  95 us

profile of v2, /device:TPU:1, one launch (start us, length us, event | category | flops | bytes accessed | tf_op | source)
XLA Modules:
  0.0 97.2 jit_solution(7367732865001641739)
XLA Ops:
  0.6 95.0 %shard_map.59 = (f32[64,512]{1,0:T(8,128)}, f32[64,128]{1,0:T(8,128)}) custom-call(f32[512,512]{1,0:T(8,128)} %samples.1, f32[64,512]{1,0:T(8,128)} %bitcast.5, f32[4096,512]{1,0:T(8,128)} %centres.1, f32[64,4096]{1,0:T(8,128)} %bitcast.4), custom_call_target="tpu_custom_call" | custom-call | tf_op jit(solution)/shard_map/pallas_call | solution.py:518
  95.6 1.6 %shard_map.60 = (f32[64,512]{1,0:T(8,128)}, f32[64,128]{1,0:T(8,128)}) custom-call(f32[64,512]{1,0:T(8,128)} %get-tuple-element.6.res_in, f32[64,128]{1,0:T(8,128)} %get-tuple-element.7.new_in), custom_call_target="tpu_custom_call" | custom-call | tf_op jit(solution)/shard_map/pallas_call | solution.py:545

commit v3 on v2

--- a/solution.py
+++ b/solution.py
@@ -263,8 +263,6 @@
                 rows.at[PLACE[(0, 1)], 0], rows.at[j, 0], row_send.at[PLACE[(dx, 1)]], row_recv.at[j],
                 (d, centre_of(dx, 0)),
             ).start()
-        await_relayed(0)
-        forward_rows(PLACE[(2, 0)])
         got(rows.at[1, 0], fwd_recv.at[1])
         got(rows.at[2, 0], fwd_recv.at[2])
 
@@ -279,7 +277,7 @@
 
         @functools.partial(loop, 0, 4)
         def _(t):
-            dy = (t + 1) % 4
+            dy = 2 - t + 3 * (t // 2) - 2 * (t // 3)
             at = pl.ds(pl.multiple_of(dy * 512, 512), 512)
             a = jnp.dot(lhs_r[...], kh[:, at], preferred_element_type=f32)
             b = jnp.dot(lhs_r[64:128, :], kl[:, at], preferred_element_type=f32)
@@ -287,9 +285,9 @@
 
             @pl.when(t < 3)
             def _():
-                remote(gpart.at[dy, top], g_y.at[t], gy_send.at[t], gy_recv.at[t], at_y(t + 1)).start()
-
-        for j in (1, 2, 3):
+                remote(gpart.at[dy, top], g_y.at[dy - 1], gy_send.at[dy - 1], gy_recv.at[dy - 1], at_y(dy)).start()
+
+        for j in (2, 1, 3):
             remote(
                 gpart.at[:, low, pl.ds(j * n, n)], h_z.at[j - 1], hz_send.at[j - 1], hz_recv.at[j - 1], at_z(j)
             ).start()
@@ -301,7 +299,7 @@
     start = pl.ds(0, n)
 
     def spread_first(it):
-        for j in (1, 2, 3):
+        for j in (2, 1, 3):
             to = 4 - j
             remote(
                 whole.at[it, 0, first, start], whole.at[it, 0, first, pl.ds(to * n, n)],
@@ -315,7 +313,7 @@
     def spread_more(it):
         for j in (1, 2, 3):
             got(whole.at[it, 0, rest, start], a_recv.at[it, j + 2])
-        for j in (1, 2, 3):
+        for j in (2, 1, 3):
             to = 4 - j
             remote(
                 whole.at[it, :, rest, start], whole.at[it, :, rest, pl.ds(to * n, n)],
@@ -323,7 +321,7 @@
             ).start()
         for j in (1, 2, 3):
             got(whole.at[it, 0, first, start], a_recv.at[it, j - 1])
-        for j in (1, 2, 3):
+        for j in (2, 1, 3):
             remote(
                 whole.at[it, 0, first], whole.at[it, 4 - j, first],
                 b_send.at[it, j + 2], b_recv.at[it, j + 2], at_y(j),
@@ -333,14 +331,14 @@
         for j in range(3):
             got(g_y.at[j], gy_recv.at[j])
         gsum[...] = gpart[0, 0:SUM_TOP] + g_y[0] + g_y[1] + g_y[2]
-        for j in (1, 2, 3):
+        for j in (2, 1, 3):
             remote(
                 gsum.at[:, pl.ds(j * n, n)], g_z.at[j - 1], gz_send.at[j - 1], gz_recv.at[j - 1], at_z(j)
             ).start()
         for j in range(3):
             got(h_z.at[j], hz_recv.at[j])
         hsum[...] = gpart[:, SUM_TOP:64, 0:n] + h_z[0] + h_z[1] + h_z[2]
-        for j in (1, 2, 3):
+        for j in (2, 1, 3):
             remote(hsum.at[j], h_y.at[j - 1], hy_send.at[j - 1], hy_recv.at[j - 1], at_y(j)).start()
         for j in range(3):
             got(g_z.at[j], gz_recv.at[j])
@@ -378,6 +376,11 @@
         pl.when(j == 0)(residuals)
         pl.when(j == 2)(gradients)
 
+        @pl.when(j == 1)
+        def _():
+            await_relayed(0)
+            forward_rows(PLACE[(2, 0)])
+
         @pl.when(j == 3)
         def _():
             pass_on(LATER_ROWS, 1)
@@ -412,10 +415,10 @@
             lhs_u[64:128, :] = hi
             k = pl.ds(pl.multiple_of(dy * 512, 512), 512)
 
-            @functools.partial(loop, 0, 4)
+            @functools.partial(loop, 0, 2)
             def _(back):
-                i = 3 - back
-                at = pl.ds(pl.multiple_of(i * 512, 512), 512)
+                i = 1 - back
+                at = pl.ds(pl.multiple_of(i * 1024, 1024), 1024)
                 a = jnp.dot(lhs_u[...], th[k, at], preferred_element_type=f32)
                 b = jnp.dot(lhs_u[64:144, :], tl[k, at], preferred_element_type=f32)
                 part[it, 0:64, at] += a[0:64] + a[64:128] + b[0:64]
@@ -428,10 +431,10 @@
                         largest = whole[1, 0, 64:72, 0:n]
                         for e in range(1, 16):
                             largest = jnp.maximum(largest, whole[1, e // 4, 64:72, e % 4 * n : e % 4 * n + n])
-                        largest = lanes(largest, 4)
+                        largest = lanes(largest, 8)
                         part[1, 64:72, at] = largest
 
-                    for j in (2 * i + 1, 2 * i):
+                    for j in (4 * i + 3, 4 * i + 2, 4 * i + 1, 4 * i):
                         theirs = pl.ds(pl.multiple_of((2 * j + 1) * n, n), n)
                         remote(
                             part.at[it, :, theirs], other.at[it, j], c_send.at[it, j], c_recv.at[it, j], (sib, c)

time: 97.3 us -> 93.4 us (0.960)
  Pallas kernels: 96.6 us -> 92.7 us
    pallas_call x1, Pallas kernels: 95 us -> 91.1 us  [body(): pl.pallas_call(step_kernel, out_shape=(jax.ShapeDtypeStruct((64, 512), f3...]
where the time goes in v3:
time: 93.4 us; the launch traced here: 93.3 us
  Pallas kernels  92.7 us (99%)
    pallas_call x1, Pallas kernels, body(): pl.pallas_call(step_kernel, out_shape=(jax.ShapeDtypeStruct((64, 512), f3...  91.1 us

profile of v3, /device:TPU:1, one launch (start us, length us, event | category | flops | bytes accessed | tf_op | source)
XLA Modules:
  0.0 93.3 jit_solution(10183578342505308410)
XLA Ops:
  0.6 91.1 %shard_map.59 = (f32[64,512]{1,0:T(8,128)}, f32[64,128]{1,0:T(8,128)}) custom-call(f32[512,512]{1,0:T(8,128)} %samples.1, f32[64,512]{1,0:T(8,128)} %bitcast.5, f32[4096,512]{1,0:T(8,128)} %centres.1, f32[64,4096]{1,0:T(8,128)} %bitcast.4), custom_call_target="tpu_custom_call" | custom-call | tf_op jit(solution)/shard_map/pallas_call | solution.py:521
  91.7 1.6 %shard_map.60 = (f32[64,512]{1,0:T(8,128)}, f32[64,128]{1,0:T(8,128)}) custom-call(f32[64,512]{1,0:T(8,128)} %get-tuple-element.6.res_in, f32[64,128]{1,0:T(8,128)} %get-tuple-element.7.new_in), custom_call_target="tpu_custom_call" | custom-call | tf_op jit(solution)/shard_map/pallas_call | solution.py:548

commit v4 on v3

--- a/solution.py
+++ b/solution.py
@@ -201,14 +201,17 @@
         both = pacc[kk * 512 : kk * 512 + 512, :].T
         pred[kk] = both[0:64] + both[64:128]
 
-        @functools.partial(loop, 1 - kk, 8)
-        def _(half):
-            s = 2 * half + kk
+        @functools.partial(loop, 0, 8)
+        def _(t):
+            s = (t + 4) % 8 * 2 + kk
             to, at_d, _ = member(s)
-            remote(
-                pred.at[kk, pl.ds(pl.multiple_of(to * 8, 8), 8)],
-                pred_in.at[s - 1], p_send.at[s - 1], p_recv.at[s - 1], (at_d, to),
-            ).start()
+
+            @pl.when(s > 0)
+            def _():
+                remote(
+                    pred.at[kk, pl.ds(pl.multiple_of(to * 8, 8), 8)],
+                    pred_in.at[s - 1], p_send.at[s - 1], p_recv.at[s - 1], (at_d, to),
+                ).start()
 
     tn = 1024
     pacc[...] = jnp.zeros_like(pacc)
@@ -252,10 +255,14 @@
             total += pred_in[s]
         res[0, mine, :] = total
 
-        @functools.partial(loop, 1, 16)
-        def _(s):
+        @functools.partial(loop, 0, 16)
+        def _(t):
+            s = (t + 8) % 16
             to, at_d, kk = member(s)
-            remote(res.at[0, mine], res.at[kk, mine], q_send.at[s - 1], q_recv.at[s - 1], (at_d, to)).start()
+
+            @pl.when(s > 0)
+            def _():
+                remote(res.at[0, mine], res.at[kk, mine], q_send.at[s - 1], q_recv.at[s - 1], (at_d, to)).start()
 
         for dx in (1, 3):
             j = PLACE[(4 - dx, 1)]
@@ -295,10 +302,11 @@
         got(rows.at[3, 0], fwd_recv.at[3])
         got(rows.at[4, 0], fwd_recv.at[4])
 
-    first, rest = pl.ds(0, TOP), pl.ds(TOP, 72 - TOP)
+    first, rests = pl.ds(0, TOP), (pl.ds(TOP, 64 - TOP), pl.ds(TOP, 72 - TOP))
     start = pl.ds(0, n)
 
     def spread_first(it):
+        rest = rests[it]
         for j in (2, 1, 3):
             to = 4 - j
             remote(
@@ -311,6 +319,7 @@
             ).start()
 
     def spread_more(it):
+        rest = rests[it]
         for j in (1, 2, 3):
             got(whole.at[it, 0, rest, start], a_recv.at[it, j + 2])
         for j in (2, 1, 3):
@@ -345,7 +354,6 @@
             got(h_y.at[j], hy_recv.at[j])
         whole[0, 0, 0:SUM_TOP, 0:n] = gsum[:, 0:n] + g_z[0] + g_z[1] + g_z[2]
         whole[0, 0, SUM_TOP:64, 0:n] = hsum[0] + h_y[0] + h_y[1] + h_y[2]
-        whole[0, 0, 64:72, 0:n] = jnp.zeros((8, n), f32)
         spread_first(0)
         got(rows.at[5, 0], fwd_recv.at[5])
 
@@ -401,10 +409,12 @@
         def _(t):
             dy = near_first(t)
 
-            @pl.when(t == 0)
-            def _():
-                for j in range(3):
-                    got(whole.at[0, :, rest, start], b_recv.at[it, j])
+            for turn in (0, 1):
+
+                @pl.when((t == 0) & (it == turn))
+                def _():
+                    for j in range(3):
+                        got(whole.at[turn, :, rests[turn], start], b_recv.at[turn, j])
 
             @pl.when(t > 0)
             def _():
@@ -496,8 +506,8 @@
         sent(h_y.at[0], hy_send.at[j])
         for it in (0, 1):
             sent(whole.at[0, 0, first, start], a_send.at[it, j])
-            sent(whole.at[0, 0, rest, start], a_send.at[it, j + 3])
-            sent(whole.at[0, :, rest, start], b_send.at[it, j])
+            sent(whole.at[0, 0, rests[it], start], a_send.at[it, j + 3])
+            sent(whole.at[0, :, rests[it], start], b_send.at[it, j])
             sent(whole.at[0, 0, first], b_send.at[it, j + 3])
 
     @functools.partial(loop, 0, 8)

time: 93.4 us -> 93.4 us (level)
  no operation moved by 1% of the time
where the time goes in v4:
time: 93.4 us; the launch traced here: 93.3 us
  Pallas kernels  92.7 us (99%)
    pallas_call x1, Pallas kernels, body(): pl.pallas_call(step_kernel, out_shape=(jax.ShapeDtypeStruct((64, 512), f3...  91.1 us

profile of v4, /device:TPU:1, one launch (start us, length us, event | category | flops | bytes accessed | tf_op | source)
XLA Modules:
  0.0 93.3 jit_solution(18164896218756703590)
XLA Ops:
  0.6 91.1 %shard_map.59 = (f32[64,512]{1,0:T(8,128)}, f32[64,128]{1,0:T(8,128)}) custom-call(f32[512,512]{1,0:T(8,128)} %samples.1, f32[64,512]{1,0:T(8,128)} %bitcast.5, f32[4096,512]{1,0:T(8,128)} %centres.1, f32[64,4096]{1,0:T(8,128)} %bitcast.4), custom_call_target="tpu_custom_call" | custom-call | tf_op jit(solution)/shard_map/pallas_call | solution.py:531
  91.7 1.6 %shard_map.60 = (f32[64,512]{1,0:T(8,128)}, f32[64,128]{1,0:T(8,128)}) custom-call(f32[64,512]{1,0:T(8,128)} %get-tuple-element.6.res_in, f32[64,128]{1,0:T(8,128)} %get-tuple-element.7.new_in), custom_call_target="tpu_custom_call" | custom-call | tf_op jit(solution)/shard_map/pallas_call | solution.py:558
